TPU v7x, 32 devices: a whole 2x2x4 slice. The times are simulated.
32 devices in a mesh: grp: 4 (over y, core), leaf: 8 (over z, x).
Axes of the slice: x: 2, y: 2, z: 4, core: 2. Of those that a mesh axis runs over, the one named last changes fastest.
Arguments:
- points: bfloat16 [131072, 64], P(('grp', 'leaf')), may hold values from -6 to 6
- solution: float32 [131072, 64], P(('grp', 'leaf')), may hold values from -6 to 6
- residual: float32 [131072, 64], P(('grp', 'leaf')), may hold values from -150 to 150
- direction: float32 [131072, 64], P(('grp', 'leaf')), may hold values from -150 to 150
- near: int32 [128, 3], P(('grp', 'leaf')), may hold values from -1 to 127, as said below
- bases: bfloat16 [128, 1024, 256], P(('grp', 'leaf')), may hold values from -0.1875 to 0.1875
- leaf_transfer: bfloat16 [128, 256, 256], P(('grp', 'leaf')), may hold values from -0.1875 to 0.1875
- inner_transfer: bfloat16 [3, 2, 256, 256], replicated, may hold values from -1 to 1
- inner_coupling: bfloat16 [3, 256, 256], replicated, may hold values from -1 to 1
- outer_transfer: bfloat16 [2, 2, 256, 256], replicated, may hold values from -1 to 1
- outer_coupling: bfloat16 [2, 256, 256], replicated, may hold values from -1 to 1
Outputs:
- new_solution: float32 [131072, 64], P(('grp', 'leaf'))
- new_residual: float32 [131072, 64], P(('grp', 'leaf'))
- new_direction: float32 [131072, 64], P(('grp', 'leaf'))
Inputs may be any that keep to these rules, and one draw needn't show every extreme that they name: Row i of near is (i, i - 1 or -1, i + 1 or -1); leaf i lists i + 1 exactly when leaf i + 1 lists i; the last leaf of each aligned block of 4 leaves lists the next leaf whenever there is one.
All inputs are finite; a program needn't handle non-finite values.
Results may differ from a plain program's by a relative error of at most 0.0027.
Values may be sent and summed in bfloat16 or wider, within the bound.
A program may use at most 128 MiB of HBM per device.

v0:
```python
import jax
import jax.numpy as jnp
from jax import lax
from jax.sharding import PartitionSpec as P

highest = lax.Precision.HIGHEST
ridge = 2.0


def padded(cells, sides, width):
    for axis, dim in sides:
        count = lax.axis_size(axis)
        ends = count - 1
        head = lax.slice_in_dim(cells, 0, width, axis=dim)
        tail = lax.slice_in_dim(cells, cells.shape[dim] - width, cells.shape[dim], axis=dim)
        cells = jnp.concatenate(
            [
                lax.ppermute(tail, axis, [(i, (i + 1) % count) for i in range(ends)]),
                cells,
                lax.ppermute(head, axis, [((i + 1) % count, i) for i in range(ends)]),
            ],
            axis=dim,
        )
    return cells


def swapped(value, axis, stride):
    return lax.ppermute(value, axis, [(i, i ^ 1 << stride) for i in range(lax.axis_size(axis))])


def kernel_block(own, window, mask):
    own_wide = own.astype(jnp.float32)
    win_wide = window.astype(jnp.float32)
    sq_own = jnp.sum(own_wide * own_wide, axis=1)
    sq_win = jnp.sum(win_wide * win_wide, axis=1)
    cross = jnp.dot(own, window.T, preferred_element_type=jnp.float32)
    dist = sq_own[:, None] + sq_win[None, :] - 2.0 * cross
    return (jnp.exp(-dist * (2.0 / own.shape[1])) * mask[None, :]).astype(jnp.bfloat16)


def couple(other, side, q_level, b_level):
    left_first = side == 0
    q_mine = jnp.where(left_first, q_level[0], q_level[1])
    coupling_mat = jnp.where(left_first, b_level, b_level.T)
    return (q_mine, jnp.dot(coupling_mat, other, precision=highest))


def join_pair(own, other, side, q_level):
    left_first = side == 0
    q_mine = jnp.where(left_first, q_level[0], q_level[1])
    q_other = jnp.where(left_first, q_level[1], q_level[0])
    return jnp.dot(q_mine.T, own, precision=highest) + jnp.dot(q_other.T, other, precision=highest)


def flag_of(value):
    return jnp.where(value >= 0, 1.0, 0.0).astype(jnp.float32)


def body(
    points,
    solution,
    residual,
    direction,
    near,
    bases,
    leaf_transfer,
    inner_transfer,
    inner_coupling,
    outer_transfer,
    outer_coupling,
):
    leaf_dev = near.shape[0]
    leaf = bases.shape[1]
    dim = points.shape[1]
    nrhs = direction.shape[1]
    packed = direction.astype(jnp.bfloat16)
    joined = jnp.concatenate([points, packed], axis=1)
    extended = padded(joined, ((("grp", "leaf"), 0),), leaf)
    vectors = packed.reshape(leaf_dev, leaf, nrhs)
    skel = jnp.einsum("lpr,lpc->lrc", bases, vectors, preferred_element_type=jnp.float32)
    trans = leaf_transfer.astype(jnp.float32)
    node = jnp.einsum("lba,lbc->ac", trans, skel, precision=highest)
    inner_q = inner_transfer.astype(jnp.float32)
    inner_b = inner_coupling.astype(jnp.float32)
    outer_q = outer_transfer.astype(jnp.float32)
    outer_b = outer_coupling.astype(jnp.float32)
    records = []
    for level in range(inner_q.shape[0]):
        other = swapped(node, "leaf", level)
        side = lax.axis_index("leaf") >> level & 1
        records.append(couple(other, side, inner_q[level], inner_b[level]))
        node = join_pair(node, other, side, inner_q[level])
    for level in range(outer_q.shape[0]):
        other = swapped(node, "grp", level)
        side = lax.axis_index("grp") >> level & 1
        records.append(couple(other, side, outer_q[level], outer_b[level]))
        node = join_pair(node, other, side, outer_q[level])
    outputs = []
    for local in range(leaf_dev):
        window = extended[local * leaf : (local + 3) * leaf]
        own = points[local * leaf : (local + 1) * leaf]
        flags = near[local]
        blocks = jnp.stack([flag_of(flags[1]), jnp.ones((), jnp.float32), flag_of(flags[2])])
        mask = jnp.repeat(blocks, leaf)
        kern = kernel_block(own, window[:, :dim], mask)
        outputs.append(jnp.dot(kern, window[:, dim:], preferred_element_type=jnp.float32))
    near_term = jnp.concatenate(outputs, axis=0)
    incoming = jnp.zeros((node.shape[0], nrhs), jnp.float32)
    for q_mine, mine in reversed(records):
        incoming = mine + jnp.dot(q_mine, incoming, precision=highest)
    leaf_in = jnp.einsum("lab,bc->lac", trans, incoming, precision=highest).astype(jnp.bfloat16)
    far_term = jnp.einsum(
        "lpr,lrc->lpc", bases, leaf_in, preferred_element_type=jnp.float32
    ).reshape(-1, nrhs)
    image = ridge * direction + near_term + far_term
    rr, pq, rq, qq = lax.psum(
        (
            jnp.sum(residual * residual, axis=0),
            jnp.sum(direction * image, axis=0),
            jnp.sum(residual * image, axis=0),
            jnp.sum(image * image, axis=0),
        ),
        ("grp", "leaf"),
    )
    alpha = rr / pq
    new_solution = solution + alpha * direction
    new_residual = residual - alpha * image
    fresh = rr - 2.0 * alpha * rq + alpha * alpha * qq
    new_direction = new_residual + fresh / rr * direction
    return (new_solution, new_residual, new_direction)


def solution(mesh):
    in_specs = (
        P(("grp", "leaf"), None),
        P(("grp", "leaf"), None),
        P(("grp", "leaf"), None),
        P(("grp", "leaf"), None),
        P(("grp", "leaf"), None),
        P(("grp", "leaf"), None, None),
        P(("grp", "leaf"), None, None),
        P(),
        P(),
        P(),
        P(),
    )
    out_specs = (P(("grp", "leaf"), None), P(("grp", "leaf"), None), P(("grp", "leaf"), None))
    return jax.shard_map(body, mesh=mesh, in_specs=in_specs, out_specs=out_specs, check_vma=False)
```

profile of v0, /device:TPU:0, one launch (start us, length us, event | category | flops | bytes accessed | tf_op | source)
XLA Modules:
  0.0 146.2 jit_solution(7510675981744808651)
XLA Ops:
  0.7 1.4 convert_element_type.59
  3.0 1.0 fusion.103
  4.0 3.0 %collective-permute-start.2 = (f32[256,64]{0,1:T(8,128)}, f32[256,64]{0,1:T(8,128)}, u32[]{:S(2)}, u32[]{:S(2)}) collective-permute-start(f32[256,64]{0,1:T(8,128)} %bitcast.13), channel_id=1, source_target_pairs={{0,1},{1,0},{2,3},{3,2},{4,5},{5,4},{6,7},{7,6},{8,9},{9,8},{10,11... | collective-permute-start | bytes 196616 | tf_op jit(solution)/shard_map/ppermute | solution.py:28
  7.0 0.8 pad_maximum_fusion.14
  7.8 2.6 %collective-permute-start = (bf16[1024,128]{0,1:T(8,128)(2,1)}, bf16[1024,128]{0,1:T(8,128)(2,1)}, u32[]{:S(2)}, u32[]{:S(2)}) collective-permute-start(bf16[1024,128]{0,1:T(8,128)(2,1)} %get-tuple-element.26), channel_id=1, source_target_pairs={{0,1},{1,2},{2,3},{3,4},{4,5},{5,6},{6,7},{7,8},{8,9},{9,10},{10,1... | collective-permute-start | bytes 786440 | tf_op jit(solution)/shard_map/ppermute | solution.py:18
  10.4 1.3 collective-permute-start.1
  11.7 0.7 multiply_reduce_fusion.11
  12.5 2.5 %convert_element_type.72 = f32[3,2,256,256]{3,2,1,0:T(8,128)} convert(bf16[3,2,256,256]{3,2,1,0:T(8,128)(2,1)} %param.18) | non-fusion elementwise | flops 393216 | bytes 2359296 | tf_op jit(solution)/shard_map/convert_element_type | solution.py:83
  14.9 2.1 %convert_element_type.74 = f32[2,2,256,256]{3,2,1,0:T(8,128)} convert(bf16[2,2,256,256]{3,2,1,0:T(8,128)(2,1)} %param.20) | non-fusion elementwise | flops 262144 | bytes 1572864 | tf_op jit(solution)/shard_map/convert_element_type | solution.py:85
  17.1 0.8 copy-done.6
  17.9 0.7 slice_bitcast_fusion.1
  18.6 1.8 %copy.18 = f32[256,256]{0,1:T(8,128)} copy(f32[256,256]{1,0:T(8,128)} %get-tuple-element.31) | data formatting | bytes 524288 | tf_op jit(solution)/shard_map/squeeze | solution.py:96
  20.4 0.8 copy.17
  21.2 1.1 convert_element_type.71
  22.3 0.9 copy-done.4
  23.2 0.9 slice_bitcast_fusion.4
  24.0 1.8 %copy.16 = f32[256,256]{0,1:T(8,128)} copy(f32[256,256]{1,0:T(8,128)} %get-tuple-element.28) | data formatting | bytes 524288 | tf_op jit(solution)/shard_map/squeeze | solution.py:91
  25.8 0.8 copy.15
  26.7 1.1 copy.14
  34.6 1.9 %fusion.50 = f32[256,64]{0,1:T(8,128)} fusion(f32[3,2,256,256]{3,2,1,0:T(8,128)} %convert_element_type.72, pred[]{:T(512)S(6)} %eq.19, f32[64,256,1]{1,0,2:T(8,128)} %fusion.103), kind=kOutput, calls=%fused_computation.92 | convolution fusion | flops 50397184 | bytes 655361 | tf_op jit(solution)/shard_map/dot_general | solution.py:52
  36.6 1.4 fusion.29
  39.3 0.7 broadcast_in_dim.11
  40.6 0.7 broadcast_in_dim.12
  41.9 1.4 convolution_add_fusion.8
  43.3 4.5 %collective-permute-start.3 = (f32[256,64]{0,1:T(8,128)S(1)}, f32[256,64]{0,1:T(8,128)S(1)}, u32[]{:S(2)}, u32[]{:S(2)}) collective-permute-start(f32[256,64]{0,1:T(8,128)S(1)} %convolution_add_fusion.8), channel_id=1, source_target_pairs={{0,2},{1,3},{2,0},{3,1},{4,6},{5,7},{6,4},{7,5},{8,10},{9,11},{10,... | collective-permute-start | bytes 196616 | tf_op jit(solution)/shard_map/ppermute | solution.py:28
  47.8 1.3 fusion.45
  49.1 1.1 collective-permute-done.3
  50.2 1.3 convolution_add_fusion.7
  51.5 2.9 %collective-permute-start.4 = (f32[256,64]{0,1:T(8,128)S(1)}, f32[256,64]{0,1:T(8,128)S(1)}, u32[]{:S(2)}, u32[]{:S(2)}) collective-permute-start(f32[256,64]{0,1:T(8,128)S(1)} %convolution_add_fusion.7), channel_id=1, source_target_pairs={{0,4},{1,5},{2,6},{3,7},{4,0},{5,1},{6,2},{7,3},{8,12},{9,13},{10,... | collective-permute-start | bytes 196616 | tf_op jit(solution)/shard_map/ppermute | solution.py:28
  54.5 1.3 fusion.40
  55.8 1.3 collective-permute-done.4
  57.1 1.3 convolution_add_fusion.6
  59.8 1.2 convolution_add_fusion.1
  61.1 4.0 %collective-permute-start.6 = (f32[256,64]{1,0:T(8,128)}, f32[256,64]{1,0:T(8,128)}, u32[]{:S(2)}, u32[]{:S(2)}) collective-permute-start(f32[256,64]{1,0:T(8,128)} %convolution_add_fusion.1), channel_id=1, source_target_pairs={{0,16},{8,24},{16,0},{24,8},{1,17},{9,25},{17,1},{25,9},{2,18},{10... | collective-permute-start | bytes 196616 | tf_op jit(solution)/shard_map/ppermute | solution.py:28
  65.1 2.0 %multiply_reduce_fusion.7 = (f32[3072]{0:T(1024)}, f32[3072]{0:T(1024)}, f32[3072]{0:T(1024)}, f32[3072]{0:T(1024)S(1)}) fusion(bf16[4096,64]{0,1:T(8,128)(2,1)S(1)} %convert_element_type.59, bf16[4096,64]{0,1:T(8,128)(2,1)S(1)} %copy-done.1, bf16[1024,128]{0,1:T(8,128)(2,1)} %collective-permute-done, bf16[1024,128]{0,1:T(8,128)(2,1)} %collective-permute-done.1), kind=kLoop, calls=%fused_computation.43 | loop fusion | flops 4313088 | bytes 2408448 | tf_op jit(solution)/shard_map/reduce_sum | solution.py:35
  67.0 6.0 %fusion.10 = f32[1024,64]{0,1:T(8,128)} fusion(f32[3072]{0:T(1024)} %mul.164, f32[3072]{0:T(1024)} %get-tuple-element.13, f32[1024]{0:T(1024)} %get-tuple-element.11, bf16[4096,64]{0,1:T(8,128)(2,1)S(1)} %convert_element_type.59, bf16[4096,64]{0,1:T(8,128)(2,1)S(1)} %copy-done.1), kind=kOutput, calls=%fused_computation.14 | convolution fusion | flops 827326464 | bytes 1208320 | tf_op jit(solution)/shard_map/dot_general | solution.py:106
  73.0 6.5 %fusion.12 = f32[1024,64]{0,1:T(8,128)} fusion(f32[3072]{0:T(1024)} %mul.157, f32[3072]{0:T(1024)} %get-tuple-element.7, f32[1024]{0:T(1024)S(1)} %copy-done.24, bf16[1024,128]{0,1:T(8,128)(2,1)} %collective-permute-done, bf16[4096,64]{0,1:T(8,128)(2,1)S(1)} %convert_element_type.59, bf16[4096,64]{0,1:T(8,128)(2,1)S(1)} %copy-done.1), kind=kOutput, calls=%fused_computation.16 | convolution fusion | flops 829685760 | bytes 3043328 | tf_op jit(solution)/shard_map/dot_general | solution.py:106
  79.6 6.4 %fusion.13 = f32[1024,64]{0,1:T(8,128)} fusion(f32[3072]{0:T(1024)} %mul.179, f32[3072]{0:T(1024)} %get-tuple-element.8, f32[1024]{0:T(1024)} %get-tuple-element.12, bf16[1024,128]{0,1:T(8,128)(2,1)} %collective-permute-done.1, bf16[4096,64]{0,1:T(8,128)(2,1)S(1)} %convert_element_type.59, bf16[4096,64]{0,1:T(8,128)(2,1)S(1)} %copy-done.1), kind=kOutput, calls=%fused_computation.17 | convolution fusion | flops 829685760 | bytes 3043328 | tf_op jit(solution)/shard_map/dot_general | solution.py:106
  86.0 6.0 %fusion.11 = f32[1024,64]{0,1:T(8,128)} fusion(f32[3072]{0:T(1024)} %mul.171, f32[3072]{0:T(1024)S(1)} %get-tuple-element.14, f32[1024]{0:T(1024)S(1)} %copy-done.23, bf16[4096,64]{0,1:T(8,128)(2,1)S(1)} %convert_element_type.59, bf16[4096,64]{0,1:T(8,128)(2,1)S(1)} %copy-done.1), kind=kOutput, calls=%fused_computation.15 | convolution fusion | flops 827326464 | bytes 1208320 | tf_op jit(solution)/shard_map/dot_general | solution.py:106
  92.0 1.6 %convolution_add_fusion = f32[256,64]{1,0:T(8,128)S(1)} fusion(f32[256,64]{1,0:T(8,128)S(1)} %fusion.29, f32[256,64]{1,0:T(8,128)} %collective-permute-done.6, f32[256,256]{0,1:T(8,128)} %copy.18, pred[]{:T(512)S(6)} %eq.23, f32[2,256,256]{2,1,0:T(8,128)} %copy-done.6), kind=kOutput, calls=%fused_computation.21 | convolution fusion | flops 50413568 | bytes 786433 | tf_op jit(solution)/shard_map/dot_general | solution.py:45
  93.6 1.4 fusion.33
  95.1 1.4 convolution_add_fusion.2
  96.9 1.3 convolution_add_fusion.3
  99.6 1.2 fusion.15
  101.5 0.7 convolution_bitcast_fusion
  103.3 1.5 %multiply_reduce_fusion.1 = (f32[64]{0:T(128)S(1)}, f32[64]{0:T(128)S(1)}, f32[64]{0:T(128)S(1)}, f32[64]{0:T(128)S(1)}, f32[4096,64]{0,1:T(8,128)}) fusion(f32[4096,64]{0,1:T(8,128)S(1)} %copy-done.8, f32[4096,64]{0,1:T(8,128)S(1)} %copy-done.3, f32[4096,64]{0,1:T(8,128)S(1)} %bitcast.152, f32[1024,64]{0,1:T(8,128)S(1)} %copy-done.15, ...), kind=kLoop, calls=%fused_computation.35 | loop fusion | flops 3669760 | bytes 5243904 | tf_op jit(solution)/shard_map/reduce_sum | solution.py:120
  104.8 37.6 %all-reduce = (f32[64]{0:T(128)S(1)}, f32[64]{0:T(128)S(1)}, f32[64]{0:T(128)S(1)}, f32[64]{0:T(128)S(1)}) all-reduce(f32[64]{0:T(128)S(1)} %get-tuple-element.6, f32[64]{0:T(128)S(1)} %get-tuple-element.5, f32[64]{0:T(128)S(1)} %get-tuple-element.4, f32[64]{0:T(128)S(1)} %get-tuple-element.3), channel_id=1, replica_groups=mesh['grp'=4,'leaf'=8] {'grp','leaf'}, use_global_device_ids=true, to_apply=%region_1.2 | all-reduce | flops 256 | bytes 2048 | tf_op jit(solution)/shard_map/psum | solution.py:116
  142.4 3.8 %multiply_add_fusion = (f32[4096,64]{0,1:T(8,128)}, f32[4096,64]{0,1:T(8,128)}, f32[4096,64]{0,1:T(8,128)}) fusion(f32[4096,64]{0,1:T(8,128)S(1)} %copy-done.3, f32[64]{0:T(128)S(1)} %get-tuple-element.21, f32[4096,64]{0,1:T(8,128)} %param.13, f32[4096,64]{0,1:T(8,128)} %get-tuple-element.23, f32[64]{0:T(128)S(1)} %get-tuple-element.22, f32[4096,64]{0,1:T(8,128)} %param.12), kind=kLoop, calls=%fused_computation.33 | loop fusion | flops 1572864 | bytes 7340544 | tf_op jit(solution)/shard_map/add | solution.py:129
  (73 shorter events, 10.2 us)
Async XLA Ops:
  0.6 1.9 %copy-start = (bf16[4,1024,256]{2,1,0:T(8,128)(2,1)S(1)}, bf16[4,1024,256]{2,1,0:T(8,128)(2,1)}, u32[]{:S(2)}) copy-start(bf16[4,1024,256]{2,1,0:T(8,128)(2,1)} %param.16) | copy-start | bytes 6291460
  0.6 2.4 %copy-start.9 = (bf16[4,256,256]{2,1,0:T(8,128)(2,1)S(1)}, bf16[4,256,256]{2,1,0:T(8,128)(2,1)}, u32[]{:S(2)}) copy-start(bf16[4,256,256]{2,1,0:T(8,128)(2,1)} %param.17) | copy-start | bytes 1572868
  2.1 4.9 %copy-start.1 = (bf16[4096,64]{0,1:T(8,128)(2,1)S(1)}, bf16[4096,64]{0,1:T(8,128)(2,1)}, u32[]{:S(2)}) copy-start(bf16[4096,64]{0,1:T(8,128)(2,1)} %param.11) | copy-start | bytes 1572868
  4.0 37.9 %collective-permute-start.2 = (f32[256,64]{0,1:T(8,128)}, f32[256,64]{0,1:T(8,128)}, u32[]{:S(2)}, u32[]{:S(2)}) collective-permute-start(f32[256,64]{0,1:T(8,128)} %bitcast.13), channel_id=1, source_target_pairs={{0,1},{1,0},{2,3},{3,2},{4,5},{5,4},{6,7},{7,6},{8,9},{9,8},{10,11... | collective-permute-start | bytes 196616 | tf_op jit(solution)/shard_map/ppermute | solution.py:28
  7.8 57.3 %collective-permute-start = (bf16[1024,128]{0,1:T(8,128)(2,1)}, bf16[1024,128]{0,1:T(8,128)(2,1)}, u32[]{:S(2)}, u32[]{:S(2)}) collective-permute-start(bf16[1024,128]{0,1:T(8,128)(2,1)} %get-tuple-element.26), channel_id=1, source_target_pairs={{0,1},{1,2},{2,3},{3,4},{4,5},{5,6},{6,7},{7,8},{8,9},{9,10},{10,1... | collective-permute-start | bytes 786440 | tf_op jit(solution)/shard_map/ppermute | solution.py:18
  10.4 54.6 %collective-permute-start.1 = (bf16[1024,128]{0,1:T(8,128)(2,1)}, bf16[1024,128]{0,1:T(8,128)(2,1)}, u32[]{:S(2)}, u32[]{:S(2)}) collective-permute-start(bf16[1024,128]{0,1:T(8,128)(2,1)} %get-tuple-element.25), channel_id=1, source_target_pairs={{1,0},{2,1},{3,2},{4,3},{5,4},{6,5},{7,6},{8,7},{9,8},{10,9},{11,1... | collective-permute-start | bytes 786440 | tf_op jit(solution)/shard_map/ppermute | solution.py:20
  12.5 4.6 %copy-start.12 = (bf16[2,256,256]{2,1,0:T(8,128)(2,1)S(1)}, bf16[2,256,256]{2,1,0:T(8,128)(2,1)}, u32[]{:S(2)}) copy-start(bf16[2,256,256]{2,1,0:T(8,128)(2,1)} %param.21) | copy-start | bytes 786436
  17.1 0.8 copy-start.6
  21.2 6.5 %copy-start.22 = (s32[4,3]{1,0:T(4,128)S(1)}, s32[4,3]{1,0:T(4,128)}, u32[]{:S(2)}) copy-start(s32[4,3]{1,0:T(4,128)} %param.15) | copy-start | bytes 148
  22.3 0.9 copy-start.4
  41.9 16.7 %copy-start.7 = (f32[2,2,256,256]{3,2,1,0:T(8,128)S(1)}, f32[2,2,256,256]{3,2,1,0:T(8,128)}, u32[]{:S(2)}) copy-start(f32[2,2,256,256]{3,2,1,0:T(8,128)} %convert_element_type.74) | copy-start | bytes 3145732
  43.3 6.9 %collective-permute-start.3 = (f32[256,64]{0,1:T(8,128)S(1)}, f32[256,64]{0,1:T(8,128)S(1)}, u32[]{:S(2)}, u32[]{:S(2)}) collective-permute-start(f32[256,64]{0,1:T(8,128)S(1)} %convolution_add_fusion.8), channel_id=1, source_target_pairs={{0,2},{1,3},{2,0},{3,1},{4,6},{5,7},{6,4},{7,5},{8,10},{9,11},{10,... | collective-permute-start | bytes 196616 | tf_op jit(solution)/shard_map/ppermute | solution.py:28
  50.2 8.3 %copy-start.17 = (f32[256,64]{0,1:T(8,128)}, f32[256,64]{0,1:T(8,128)S(1)}, u32[]{:S(2)}) copy-start(f32[256,64]{0,1:T(8,128)S(1)} %collective-permute-done.3) | copy-start | bytes 196612
  51.5 5.6 %collective-permute-start.4 = (f32[256,64]{0,1:T(8,128)S(1)}, f32[256,64]{0,1:T(8,128)S(1)}, u32[]{:S(2)}, u32[]{:S(2)}) collective-permute-start(f32[256,64]{0,1:T(8,128)S(1)} %convolution_add_fusion.7), channel_id=1, source_target_pairs={{0,4},{1,5},{2,6},{3,7},{4,0},{5,1},{6,2},{7,3},{8,12},{9,13},{10,... | collective-permute-start | bytes 196616 | tf_op jit(solution)/shard_map/ppermute | solution.py:28
  57.1 1.4 copy-start.19
  58.5 1.3 collective-permute-start.5
  59.8 1.2 copy-start.21
  61.1 31.0 %collective-permute-start.6 = (f32[256,64]{1,0:T(8,128)}, f32[256,64]{1,0:T(8,128)}, u32[]{:S(2)}, u32[]{:S(2)}) collective-permute-start(f32[256,64]{1,0:T(8,128)} %convolution_add_fusion.1), channel_id=1, source_target_pairs={{0,16},{8,24},{16,0},{24,8},{1,17},{9,25},{17,1},{25,9},{2,18},{10... | collective-permute-start | bytes 196616 | tf_op jit(solution)/shard_map/ppermute | solution.py:28
  67.0 6.0 %copy-start.24 = (f32[1024]{0:T(1024)S(1)}, f32[1024]{0:T(1024)}, u32[]{:S(2)}) copy-start(f32[1024]{0:T(1024)} %get-tuple-element.9) | copy-start | bytes 12292
  79.6 6.4 %copy-start.23 = (f32[1024]{0:T(1024)S(1)}, f32[1024]{0:T(1024)}, u32[]{:S(2)}) copy-start(f32[1024]{0:T(1024)} %get-tuple-element.10) | copy-start | bytes 12292
  92.0 4.4 %copy-start.2 = (f32[3,2,256,256]{3,2,1,0:T(8,128)S(1)}, f32[3,2,256,256]{3,2,1,0:T(8,128)}, u32[]{:S(2)}) copy-start(f32[3,2,256,256]{3,2,1,0:T(8,128)} %convert_element_type.72) | copy-start | bytes 4718596
  92.0 4.9 %copy-start.5 = (f32[3,256,256]{2,1,0:T(8,128)S(1)}, f32[3,256,256]{2,1,0:T(8,128)}, u32[]{:S(2)}) copy-start(f32[3,256,256]{2,1,0:T(8,128)} %copy-done.4) | copy-start | bytes 2359300
  92.0 4.9 %copy-start.20 = (f32[256,64]{0,1:T(8,128)S(1)}, f32[256,64]{0,1:T(8,128)}, u32[]{:S(2)}) copy-start(f32[256,64]{0,1:T(8,128)} %copy-done.19) | copy-start | bytes 196612
  92.0 6.6 %copy-start.11 = (f32[256,256]{0,1:T(8,128)S(1)}, f32[256,256]{0,1:T(8,128)}, u32[]{:S(2)}) copy-start(f32[256,256]{0,1:T(8,128)} %copy.15) | copy-start | bytes 786436
  92.0 6.6 %copy-start.18 = (f32[256,64]{0,1:T(8,128)S(1)}, f32[256,64]{0,1:T(8,128)}, u32[]{:S(2)}) copy-start(f32[256,64]{0,1:T(8,128)} %copy-done.17) | copy-start | bytes 196612
  96.5 4.3 %copy-start.10 = (bf16[4,256,256]{2,1,0:T(8,128)(2,1)S(1)}, bf16[4,256,256]{2,1,0:T(8,128)(2,1)}, u32[]{:S(2)}) copy-start(bf16[4,256,256]{2,1,0:T(8,128)(2,1)} %param.17) | copy-start | bytes 1572868
  101.5 1.2 copy-start.3
  101.5 1.5 %copy-start.8 = (f32[4096,64]{0,1:T(8,128)S(1)}, f32[4096,64]{0,1:T(8,128)}, u32[]{:S(2)}) copy-start(f32[4096,64]{0,1:T(8,128)} %param.13) | copy-start | bytes 3145732
  101.5 1.6 %copy-start.13 = (f32[1024,64]{0,1:T(8,128)S(1)}, f32[1024,64]{0,1:T(8,128)}, u32[]{:S(2)}) copy-start(f32[1024,64]{0,1:T(8,128)} %fusion.10) | copy-start | bytes 786436
  101.5 1.6 %copy-start.14 = (f32[1024,64]{0,1:T(8,128)S(1)}, f32[1024,64]{0,1:T(8,128)}, u32[]{:S(2)}) copy-start(f32[1024,64]{0,1:T(8,128)} %fusion.12) | copy-start | bytes 786436
  101.5 1.7 %copy-start.15 = (f32[1024,64]{0,1:T(8,128)S(1)}, f32[1024,64]{0,1:T(8,128)}, u32[]{:S(2)}) copy-start(f32[1024,64]{0,1:T(8,128)} %fusion.13) | copy-start | bytes 786436
  101.5 1.8 %copy-start.16 = (f32[1024,64]{0,1:T(8,128)S(1)}, f32[1024,64]{0,1:T(8,128)}, u32[]{:S(2)}) copy-start(f32[1024,64]{0,1:T(8,128)} %fusion.11) | copy-start | bytes 786436
where the time goes:
time: 147 us; the launch traced here: 146 us
  matrix products  48.3 us (33%)
  blocking collectives  37.6 us (26%)
  starting transfers between devices  18.4 us (13%)
  other arithmetic  17.2 us (12%)
  local copies, waits for them, and re-layouts  15.7 us (11%)
  between operations  5.92 us (4%)
  waiting for transfers between devices  3.06 us (2%)
    psum x1, blocking collectives, body(): lax.psum((jnp.sum(residual * residual, axis=0), jnp.sum(direction * image...  37.6 us
    dot_general x4, matrix products, body(): jnp.dot(kern, window[:, dim:], preferred_element_type=jnp.float32)  25 us
    ppermute x5, starting transfers between devices, swapped(): lax.ppermute(value, axis, [(i, i ^ 1 << stride) for i in range(lax.axis_s...  14.5 us
    dot_general x5, matrix products, couple(): return (q_mine, jnp.dot(coupling_mat, other, precision=highest))  6.09 us
    dot_general x4, matrix products, join_pair(): jnp.dot(q_other.T, other, precision=highest)  5.34 us
    dot_general x4, matrix products, join_pair(): jnp.dot(q_mine.T, own, precision=highest)  5.18 us
    squeeze x4, local copies, waits for them, and re-layouts, body(): records.append(couple(other, side, inner_q[level], inner_b[level]))  4.55 us
    dot_general x5, matrix products, body(): incoming = mine + jnp.dot(q_mine, incoming, precision=highest)  3.93 us
  transfers between devices with their start and end apart: 7, of which 3 were waited for; matrix products, arithmetic and copies ran while one was open for 41% of the time, Pallas kernels for 0%

commit v1 on v0

--- a/solution.py
+++ b/solution.py
@@ -5,6 +5,11 @@
 
 highest = lax.Precision.HIGHEST
 ridge = 2.0
+
+
+def axis_by_axis(array, inner_axis, outer_axis):
+    partial = lax.psum(array, inner_axis)
+    return lax.psum(partial, outer_axis)
 
 
 def padded(cells, sides, width):
@@ -113,14 +118,15 @@
         "lpr,lrc->lpc", bases, leaf_in, preferred_element_type=jnp.float32
     ).reshape(-1, nrhs)
     image = ridge * direction + near_term + far_term
-    rr, pq, rq, qq = lax.psum(
+    rr, pq, rq, qq = axis_by_axis(
         (
             jnp.sum(residual * residual, axis=0),
             jnp.sum(direction * image, axis=0),
             jnp.sum(residual * image, axis=0),
             jnp.sum(image * image, axis=0),
         ),
-        ("grp", "leaf"),
+        "leaf",
+        "grp",
     )
     alpha = rr / pq
     new_solution = solution + alpha * direction

time: 147 us -> 134 us (0.912)
  blocking collectives: 37.6 us -> 23.8 us
    psum x1 -> x2, blocking collectives: 37.6 us -> 23.8 us  [the longest x1 17.9 us: axis_by_axis(): partial = lax.psum(array, inner_axis)]
  transfers between devices with their start and end apart: 7 -> 7, of which waited for: 3 -> 3; matrix products, arithmetic and copies ran while one was open for 41% -> 45% of each run, Pallas kernels for 0% -> 0%
where the time goes in v1:
time: 134 us; the launch traced here: 133 us
  matrix products  48.3 us (36%)
  blocking collectives  23.8 us (18%)
  starting transfers between devices  18.4 us (14%)
  other arithmetic  17.2 us (13%)
  local copies, waits for them, and re-layouts  15.8 us (12%)
  between operations  6.11 us (5%)
  waiting for transfers between devices  3.06 us (2%)
    dot_general x4, matrix products, body(): jnp.dot(kern, window[:, dim:], preferred_element_type=jnp.float32)  25 us
    psum x1, blocking collectives, axis_by_axis(): partial = lax.psum(array, inner_axis)  17.9 us
    ppermute x5, starting transfers between devices, swapped(): lax.ppermute(value, axis, [(i, i ^ 1 << stride) for i in range(lax.axis_s...  14.5 us
    dot_general x5, matrix products, couple(): return (q_mine, jnp.dot(coupling_mat, other, precision=highest))  6.09 us
    psum x1, blocking collectives, axis_by_axis(): return lax.psum(partial, outer_axis)  5.86 us
    dot_general x4, matrix products, join_pair(): jnp.dot(q_other.T, other, precision=highest)  5.35 us
    dot_general x4, matrix products, join_pair(): jnp.dot(q_mine.T, own, precision=highest)  5.17 us
    squeeze x4, local copies, waits for them, and re-layouts, body(): records.append(couple(other, side, inner_q[level], inner_b[level]))  4.58 us
  transfers between devices with their start and end apart: 7, of which 3 were waited for; matrix products, arithmetic and copies ran while one was open for 45% of the time, Pallas kernels for 0%

profile of v1, /device:TPU:0, one launch (start us, length us, event | category | flops | bytes accessed | tf_op | source)
XLA Modules:
  0.0 132.7 jit_solution(14895118023645145456)
XLA Ops:
  0.7 1.4 %convert_element_type.59 = bf16[4096,64]{0,1:T(8,128)(2,1)S(1)} convert(f32[4096,64]{0,1:T(8,128)} %param.14) | non-fusion elementwise | flops 262144 | bytes 1572864 | tf_op jit(solution)/shard_map/convert_element_type | solution.py:81
  3.0 1.0 fusion.103
  4.0 3.0 %collective-permute-start.2 = (f32[256,64]{0,1:T(8,128)}, f32[256,64]{0,1:T(8,128)}, u32[]{:S(2)}, u32[]{:S(2)}) collective-permute-start(f32[256,64]{0,1:T(8,128)} %bitcast.13), channel_id=1, source_target_pairs={{0,1},{1,0},{2,3},{3,2},{4,5},{5,4},{6,7},{7,6},{8,9},{9,8},{10,11... | collective-permute-start | bytes 196616 | tf_op jit(solution)/shard_map/ppermute | solution.py:33
  7.0 0.8 pad_maximum_fusion.14
  7.8 2.6 %collective-permute-start = (bf16[1024,128]{0,1:T(8,128)(2,1)}, bf16[1024,128]{0,1:T(8,128)(2,1)}, u32[]{:S(2)}, u32[]{:S(2)}) collective-permute-start(bf16[1024,128]{0,1:T(8,128)(2,1)} %get-tuple-element.30), channel_id=1, source_target_pairs={{0,1},{1,2},{2,3},{3,4},{4,5},{5,6},{6,7},{7,8},{8,9},{9,10},{10,1... | collective-permute-start | bytes 786440 | tf_op jit(solution)/shard_map/ppermute | solution.py:23
  10.4 1.3 collective-permute-start.1
  11.7 0.7 multiply_reduce_fusion.11
  12.5 2.5 %convert_element_type.72 = f32[3,2,256,256]{3,2,1,0:T(8,128)} convert(bf16[3,2,256,256]{3,2,1,0:T(8,128)(2,1)} %param.18) | non-fusion elementwise | flops 393216 | bytes 2359296 | tf_op jit(solution)/shard_map/convert_element_type | solution.py:88
  14.9 2.1 %convert_element_type.74 = f32[2,2,256,256]{3,2,1,0:T(8,128)} convert(bf16[2,2,256,256]{3,2,1,0:T(8,128)(2,1)} %param.20) | non-fusion elementwise | flops 262144 | bytes 1572864 | tf_op jit(solution)/shard_map/convert_element_type | solution.py:90
  17.1 0.8 copy-done.6
  17.9 0.7 slice_bitcast_fusion.1
  18.6 1.8 %copy.18 = f32[256,256]{0,1:T(8,128)} copy(f32[256,256]{1,0:T(8,128)} %get-tuple-element.35) | data formatting | bytes 524288 | tf_op jit(solution)/shard_map/squeeze | solution.py:101
  20.4 0.8 copy.17
  21.2 1.1 convert_element_type.71
  22.3 0.9 copy-done.4
  23.2 0.9 slice_bitcast_fusion.4
  24.1 1.8 %copy.16 = f32[256,256]{0,1:T(8,128)} copy(f32[256,256]{1,0:T(8,128)} %get-tuple-element.32) | data formatting | bytes 524288 | tf_op jit(solution)/shard_map/squeeze | solution.py:96
  25.9 0.9 copy.15
  26.7 1.1 copy.14
  34.9 1.9 %fusion.50 = f32[256,64]{0,1:T(8,128)} fusion(f32[3,2,256,256]{3,2,1,0:T(8,128)} %convert_element_type.72, pred[]{:T(512)S(6)} %eq.19, f32[64,256,1]{1,0,2:T(8,128)} %fusion.103), kind=kOutput, calls=%fused_computation.92 | convolution fusion | flops 50397184 | bytes 655361 | tf_op jit(solution)/shard_map/dot_general | solution.py:57
  36.8 1.4 %fusion.29 = f32[256,64]{1,0:T(8,128)S(1)} fusion(f32[2,2,256,256]{3,2,1,0:T(8,128)} %convert_element_type.74, pred[]{:T(512)S(6)} %eq.23), kind=kOutput, calls=%fused_computation.61 | convolution fusion | flops 50397184 | bytes 589825 | tf_op jit(solution)/shard_map/dot_general | solution.py:115
  40.8 0.7 broadcast_in_dim.12
  42.2 1.4 %convolution_add_fusion.8 = f32[256,64]{0,1:T(8,128)S(1)} fusion(f32[256,64]{0,1:T(8,128)} %fusion.50, f32[256,64]{0,1:T(8,128)} %collective-permute-done.2, f32[3,2,256,256]{3,2,1,0:T(8,128)} %convert_element_type.72, pred[]{:T(512)S(6)} %eq.19), kind=kOutput, calls=%fused_computation.30 | convolution fusion | flops 50413568 | bytes 720897 | tf_op jit(solution)/shard_map/dot_general | solution.py:57
  43.6 4.5 %collective-permute-start.3 = (f32[256,64]{0,1:T(8,128)S(1)}, f32[256,64]{0,1:T(8,128)S(1)}, u32[]{:S(2)}, u32[]{:S(2)}) collective-permute-start(f32[256,64]{0,1:T(8,128)S(1)} %convolution_add_fusion.8), channel_id=1, source_target_pairs={{0,2},{1,3},{2,0},{3,1},{4,6},{5,7},{6,4},{7,5},{8,10},{9,11},{10,... | collective-permute-start | bytes 196616 | tf_op jit(solution)/shard_map/ppermute | solution.py:33
  48.1 1.3 fusion.45
  49.4 1.1 collective-permute-done.3
  50.5 1.3 %convolution_add_fusion.7 = f32[256,64]{0,1:T(8,128)S(1)} fusion(f32[256,64]{0,1:T(8,128)S(1)} %fusion.45, f32[256,64]{0,1:T(8,128)S(1)} %collective-permute-done.3, f32[3,2,256,256]{3,2,1,0:T(8,128)} %convert_element_type.72, pred[]{:T(512)S(6)} %eq.20), kind=kOutput, calls=%fused_computation.29 | convolution fusion | flops 50413568 | bytes 720897 | tf_op jit(solution)/shard_map/dot_general | solution.py:57
  51.8 2.9 %collective-permute-start.4 = (f32[256,64]{0,1:T(8,128)S(1)}, f32[256,64]{0,1:T(8,128)S(1)}, u32[]{:S(2)}, u32[]{:S(2)}) collective-permute-start(f32[256,64]{0,1:T(8,128)S(1)} %convolution_add_fusion.7), channel_id=1, source_target_pairs={{0,4},{1,5},{2,6},{3,7},{4,0},{5,1},{6,2},{7,3},{8,12},{9,13},{10,... | collective-permute-start | bytes 196616 | tf_op jit(solution)/shard_map/ppermute | solution.py:33
  54.8 1.3 fusion.40
  56.1 1.3 %collective-permute-done.4 = f32[256,64]{0,1:T(8,128)S(1)} collective-permute-done((f32[256,64]{0,1:T(8,128)S(1)}, f32[256,64]{0,1:T(8,128)S(1)}, u32[]{:S(2)}, u32[]{:S(2)}) %collective-permute-start.4) | collective-permute-done | bytes 65568 | tf_op jit(solution)/shard_map/ppermute | solution.py:33
  57.4 1.3 %convolution_add_fusion.6 = f32[256,64]{0,1:T(8,128)S(1)} fusion(f32[256,64]{0,1:T(8,128)S(1)} %fusion.40, f32[256,64]{0,1:T(8,128)S(1)} %collective-permute-done.4, f32[3,2,256,256]{3,2,1,0:T(8,128)} %convert_element_type.72, pred[]{:T(512)S(6)} %eq.21), kind=kOutput, calls=%fused_computation.28 | convolution fusion | flops 50413568 | bytes 720897 | tf_op jit(solution)/shard_map/dot_general | solution.py:57
  60.1 1.2 convolution_add_fusion.1
  61.4 4.0 %collective-permute-start.6 = (f32[256,64]{1,0:T(8,128)}, f32[256,64]{1,0:T(8,128)}, u32[]{:S(2)}, u32[]{:S(2)}) collective-permute-start(f32[256,64]{1,0:T(8,128)} %convolution_add_fusion.1), channel_id=1, source_target_pairs={{0,16},{8,24},{16,0},{24,8},{1,17},{9,25},{17,1},{25,9},{2,18},{10... | collective-permute-start | bytes 196616 | tf_op jit(solution)/shard_map/ppermute | solution.py:33
  65.4 2.0 %multiply_reduce_fusion.7 = (f32[3072]{0:T(1024)}, f32[3072]{0:T(1024)}, f32[3072]{0:T(1024)}, f32[3072]{0:T(1024)S(1)}) fusion(bf16[4096,64]{0,1:T(8,128)(2,1)S(1)} %convert_element_type.59, bf16[4096,64]{0,1:T(8,128)(2,1)S(1)} %copy-done.1, bf16[1024,128]{0,1:T(8,128)(2,1)} %collective-permute-done, bf16[1024,128]{0,1:T(8,128)(2,1)} %collective-permute-done.1), kind=kLoop, calls=%fused_computation.43 | loop fusion | flops 4313088 | bytes 2408448 | tf_op jit(solution)/shard_map/reduce_sum | solution.py:40
  67.3 6.0 %fusion.10 = f32[1024,64]{0,1:T(8,128)} fusion(f32[3072]{0:T(1024)} %mul.164, f32[3072]{0:T(1024)} %get-tuple-element.13, f32[1024]{0:T(1024)} %get-tuple-element.11, bf16[4096,64]{0,1:T(8,128)(2,1)S(1)} %convert_element_type.59, bf16[4096,64]{0,1:T(8,128)(2,1)S(1)} %copy-done.1), kind=kOutput, calls=%fused_computation.14 | convolution fusion | flops 827326464 | bytes 1208320 | tf_op jit(solution)/shard_map/dot_general | solution.py:111
  73.3 6.6 %fusion.12 = f32[1024,64]{0,1:T(8,128)} fusion(f32[3072]{0:T(1024)} %mul.157, f32[3072]{0:T(1024)} %get-tuple-element.7, f32[1024]{0:T(1024)S(1)} %copy-done.24, bf16[1024,128]{0,1:T(8,128)(2,1)} %collective-permute-done, bf16[4096,64]{0,1:T(8,128)(2,1)S(1)} %convert_element_type.59, bf16[4096,64]{0,1:T(8,128)(2,1)S(1)} %copy-done.1), kind=kOutput, calls=%fused_computation.16 | convolution fusion | flops 829685760 | bytes 3043328 | tf_op jit(solution)/shard_map/dot_general | solution.py:111
  79.9 6.4 %fusion.13 = f32[1024,64]{0,1:T(8,128)} fusion(f32[3072]{0:T(1024)} %mul.179, f32[3072]{0:T(1024)} %get-tuple-element.8, f32[1024]{0:T(1024)} %get-tuple-element.12, bf16[1024,128]{0,1:T(8,128)(2,1)} %collective-permute-done.1, bf16[4096,64]{0,1:T(8,128)(2,1)S(1)} %convert_element_type.59, bf16[4096,64]{0,1:T(8,128)(2,1)S(1)} %copy-done.1), kind=kOutput, calls=%fused_computation.17 | convolution fusion | flops 829685760 | bytes 3043328 | tf_op jit(solution)/shard_map/dot_general | solution.py:111
  86.3 6.0 %fusion.11 = f32[1024,64]{0,1:T(8,128)} fusion(f32[3072]{0:T(1024)} %mul.171, f32[3072]{0:T(1024)S(1)} %get-tuple-element.14, f32[1024]{0:T(1024)S(1)} %copy-done.23, bf16[4096,64]{0,1:T(8,128)(2,1)S(1)} %convert_element_type.59, bf16[4096,64]{0,1:T(8,128)(2,1)S(1)} %copy-done.1), kind=kOutput, calls=%fused_computation.15 | convolution fusion | flops 827326464 | bytes 1208320 | tf_op jit(solution)/shard_map/dot_general | solution.py:111
  92.3 1.6 %convolution_add_fusion = f32[256,64]{1,0:T(8,128)S(1)} fusion(f32[256,64]{1,0:T(8,128)S(1)} %fusion.29, f32[256,64]{1,0:T(8,128)} %collective-permute-done.6, f32[256,256]{0,1:T(8,128)} %copy.18, pred[]{:T(512)S(6)} %eq.23, f32[2,256,256]{2,1,0:T(8,128)} %copy-done.6), kind=kOutput, calls=%fused_computation.21 | convolution fusion | flops 50413568 | bytes 786433 | tf_op jit(solution)/shard_map/dot_general | solution.py:50
  93.9 1.4 %fusion.33 = f32[256,64]{1,0:T(8,128)S(1)} fusion(f32[256,64]{1,0:T(8,128)S(1)} %convolution_add_fusion, f32[2,2,256,256]{3,2,1,0:T(8,128)} %convert_element_type.74, pred[]{:T(512)S(6)} %eq.22), kind=kOutput, calls=%fused_computation.72 | convolution fusion | flops 50397184 | bytes 655361 | tf_op jit(solution)/shard_map/dot_general | solution.py:115
  95.3 1.4 %convolution_add_fusion.2 = f32[256,64]{1,0:T(8,128)S(1)} fusion(f32[256,64]{1,0:T(8,128)S(1)} %fusion.33, f32[256,64]{0,1:T(8,128)} %copy-done.21, f32[256,256]{0,1:T(8,128)} %copy.17, pred[]{:T(512)S(6)} %eq.22, f32[2,256,256]{2,1,0:T(8,128)} %copy-done.6), kind=kOutput, calls=%fused_computation.23 | convolution fusion | flops 50413568 | bytes 720897 | tf_op jit(solution)/shard_map/dot_general | solution.py:50
  97.2 1.3 convolution_add_fusion.3
  99.9 1.2 fusion.15
  101.8 0.7 convolution_bitcast_fusion
  103.6 1.5 %multiply_reduce_fusion.1 = (f32[64]{0:T(128)S(1)}, f32[64]{0:T(128)S(1)}, f32[64]{0:T(128)S(1)}, f32[64]{0:T(128)S(1)}, f32[4096,64]{0,1:T(8,128)}) fusion(f32[4096,64]{0,1:T(8,128)S(1)} %copy-done.8, f32[4096,64]{0,1:T(8,128)S(1)} %copy-done.3, f32[4096,64]{0,1:T(8,128)S(1)} %bitcast.152, f32[1024,64]{0,1:T(8,128)S(1)} %copy-done.15, ...), kind=kLoop, calls=%fused_computation.35 | loop fusion | flops 3669760 | bytes 5243904 | tf_op jit(solution)/shard_map/reduce_sum | solution.py:125
  105.1 17.9 %all-reduce = (f32[64]{0:T(128)S(1)}, f32[64]{0:T(128)S(1)}, f32[64]{0:T(128)S(1)}, f32[64]{0:T(128)S(1)}) all-reduce(f32[64]{0:T(128)S(1)} %get-tuple-element.6, f32[64]{0:T(128)S(1)} %get-tuple-element.5, f32[64]{0:T(128)S(1)} %get-tuple-element.4, f32[64]{0:T(128)S(1)} %get-tuple-element.3), channel_id=1, replica_groups=mesh['grp'=4,'leaf'=8] {'leaf'}, use_global_device_ids=true, to_apply=%region_1.2 | all-reduce | flops 256 | bytes 2048 | tf_op jit(solution)/shard_map/psum | solution.py:11
  123.0 5.9 %all-reduce.1 = (f32[64]{0:T(128)S(1)}, f32[64]{0:T(128)S(1)}, f32[64]{0:T(128)S(1)}, f32[64]{0:T(128)S(1)}) all-reduce(f32[64]{0:T(128)S(1)} %get-tuple-element.15, f32[64]{0:T(128)S(1)} %get-tuple-element.16, f32[64]{0:T(128)S(1)} %get-tuple-element.17, f32[64]{0:T(128)S(1)} %get-tuple-element.18), channel_id=1, replica_groups=mesh['grp'=4,'leaf'=8] {'grp'}, use_global_device_ids=true, to_apply=%region_2.3 | all-reduce | flops 256 | bytes 2048 | tf_op jit(solution)/shard_map/psum | solution.py:12
  128.9 3.8 %multiply_add_fusion = (f32[4096,64]{0,1:T(8,128)}, f32[4096,64]{0,1:T(8,128)}, f32[4096,64]{0,1:T(8,128)}) fusion(f32[4096,64]{0,1:T(8,128)S(1)} %copy-done.3, f32[64]{0:T(128)S(1)} %get-tuple-element.25, f32[4096,64]{0,1:T(8,128)} %param.13, f32[4096,64]{0,1:T(8,128)} %get-tuple-element.27, f32[64]{0:T(128)S(1)} %get-tuple-element.26, f32[4096,64]{0,1:T(8,128)} %param.12), kind=kLoop, calls=%fused_computation.33 | loop fusion | flops 1572864 | bytes 7340544 | tf_op jit(solution)/shard_map/add | solution.py:135
  (74 shorter events, 10.9 us)
Async XLA Ops:
  0.6 1.9 %copy-start = (bf16[4,1024,256]{2,1,0:T(8,128)(2,1)S(1)}, bf16[4,1024,256]{2,1,0:T(8,128)(2,1)}, u32[]{:S(2)}) copy-start(bf16[4,1024,256]{2,1,0:T(8,128)(2,1)} %param.16) | copy-start | bytes 6291460
  0.6 2.4 %copy-start.9 = (bf16[4,256,256]{2,1,0:T(8,128)(2,1)S(1)}, bf16[4,256,256]{2,1,0:T(8,128)(2,1)}, u32[]{:S(2)}) copy-start(bf16[4,256,256]{2,1,0:T(8,128)(2,1)} %param.17) | copy-start | bytes 1572868
  2.1 4.9 %copy-start.1 = (bf16[4096,64]{0,1:T(8,128)(2,1)S(1)}, bf16[4096,64]{0,1:T(8,128)(2,1)}, u32[]{:S(2)}) copy-start(bf16[4096,64]{0,1:T(8,128)(2,1)} %param.11) | copy-start | bytes 1572868
  4.0 38.2 %collective-permute-start.2 = (f32[256,64]{0,1:T(8,128)}, f32[256,64]{0,1:T(8,128)}, u32[]{:S(2)}, u32[]{:S(2)}) collective-permute-start(f32[256,64]{0,1:T(8,128)} %bitcast.13), channel_id=1, source_target_pairs={{0,1},{1,0},{2,3},{3,2},{4,5},{5,4},{6,7},{7,6},{8,9},{9,8},{10,11... | collective-permute-start | bytes 196616 | tf_op jit(solution)/shard_map/ppermute | solution.py:33
  7.8 57.5 %collective-permute-start = (bf16[1024,128]{0,1:T(8,128)(2,1)}, bf16[1024,128]{0,1:T(8,128)(2,1)}, u32[]{:S(2)}, u32[]{:S(2)}) collective-permute-start(bf16[1024,128]{0,1:T(8,128)(2,1)} %get-tuple-element.30), channel_id=1, source_target_pairs={{0,1},{1,2},{2,3},{3,4},{4,5},{5,6},{6,7},{7,8},{8,9},{9,10},{10,1... | collective-permute-start | bytes 786440 | tf_op jit(solution)/shard_map/ppermute | solution.py:23
  10.4 54.9 %collective-permute-start.1 = (bf16[1024,128]{0,1:T(8,128)(2,1)}, bf16[1024,128]{0,1:T(8,128)(2,1)}, u32[]{:S(2)}, u32[]{:S(2)}) collective-permute-start(bf16[1024,128]{0,1:T(8,128)(2,1)} %get-tuple-element.29), channel_id=1, source_target_pairs={{1,0},{2,1},{3,2},{4,3},{5,4},{6,5},{7,6},{8,7},{9,8},{10,9},{11,1... | collective-permute-start | bytes 786440 | tf_op jit(solution)/shard_map/ppermute | solution.py:25
  12.5 4.6 %copy-start.12 = (bf16[2,256,256]{2,1,0:T(8,128)(2,1)S(1)}, bf16[2,256,256]{2,1,0:T(8,128)(2,1)}, u32[]{:S(2)}) copy-start(bf16[2,256,256]{2,1,0:T(8,128)(2,1)} %param.21) | copy-start | bytes 786436
  17.1 0.8 copy-start.6
  21.2 6.6 %copy-start.22 = (s32[4,3]{1,0:T(4,128)S(1)}, s32[4,3]{1,0:T(4,128)}, u32[]{:S(2)}) copy-start(s32[4,3]{1,0:T(4,128)} %param.15) | copy-start | bytes 148
  22.3 0.9 copy-start.4
  42.2 16.7 %copy-start.7 = (f32[2,2,256,256]{3,2,1,0:T(8,128)S(1)}, f32[2,2,256,256]{3,2,1,0:T(8,128)}, u32[]{:S(2)}) copy-start(f32[2,2,256,256]{3,2,1,0:T(8,128)} %convert_element_type.74) | copy-start | bytes 3145732
  43.6 6.9 %collective-permute-start.3 = (f32[256,64]{0,1:T(8,128)S(1)}, f32[256,64]{0,1:T(8,128)S(1)}, u32[]{:S(2)}, u32[]{:S(2)}) collective-permute-start(f32[256,64]{0,1:T(8,128)S(1)} %convolution_add_fusion.8), channel_id=1, source_target_pairs={{0,2},{1,3},{2,0},{3,1},{4,6},{5,7},{6,4},{7,5},{8,10},{9,11},{10,... | collective-permute-start | bytes 196616 | tf_op jit(solution)/shard_map/ppermute | solution.py:33
  50.5 8.3 %copy-start.17 = (f32[256,64]{0,1:T(8,128)}, f32[256,64]{0,1:T(8,128)S(1)}, u32[]{:S(2)}) copy-start(f32[256,64]{0,1:T(8,128)S(1)} %collective-permute-done.3) | copy-start | bytes 196612
  51.8 5.6 %collective-permute-start.4 = (f32[256,64]{0,1:T(8,128)S(1)}, f32[256,64]{0,1:T(8,128)S(1)}, u32[]{:S(2)}, u32[]{:S(2)}) collective-permute-start(f32[256,64]{0,1:T(8,128)S(1)} %convolution_add_fusion.7), channel_id=1, source_target_pairs={{0,4},{1,5},{2,6},{3,7},{4,0},{5,1},{6,2},{7,3},{8,12},{9,13},{10,... | collective-permute-start | bytes 196616 | tf_op jit(solution)/shard_map/ppermute | solution.py:33
  57.4 1.4 %copy-start.19 = (f32[256,64]{0,1:T(8,128)}, f32[256,64]{0,1:T(8,128)S(1)}, u32[]{:S(2)}) copy-start(f32[256,64]{0,1:T(8,128)S(1)} %collective-permute-done.4) | copy-start | bytes 196612
  58.8 1.3 collective-permute-start.5
  60.1 1.3 copy-start.21
  61.4 31.0 %collective-permute-start.6 = (f32[256,64]{1,0:T(8,128)}, f32[256,64]{1,0:T(8,128)}, u32[]{:S(2)}, u32[]{:S(2)}) collective-permute-start(f32[256,64]{1,0:T(8,128)} %convolution_add_fusion.1), channel_id=1, source_target_pairs={{0,16},{8,24},{16,0},{24,8},{1,17},{9,25},{17,1},{25,9},{2,18},{10... | collective-permute-start | bytes 196616 | tf_op jit(solution)/shard_map/ppermute | solution.py:33
  67.3 6.0 %copy-start.24 = (f32[1024]{0:T(1024)S(1)}, f32[1024]{0:T(1024)}, u32[]{:S(2)}) copy-start(f32[1024]{0:T(1024)} %get-tuple-element.9) | copy-start | bytes 12292
  79.9 6.4 %copy-start.23 = (f32[1024]{0:T(1024)S(1)}, f32[1024]{0:T(1024)}, u32[]{:S(2)}) copy-start(f32[1024]{0:T(1024)} %get-tuple-element.10) | copy-start | bytes 12292
  92.3 4.4 %copy-start.2 = (f32[3,2,256,256]{3,2,1,0:T(8,128)S(1)}, f32[3,2,256,256]{3,2,1,0:T(8,128)}, u32[]{:S(2)}) copy-start(f32[3,2,256,256]{3,2,1,0:T(8,128)} %convert_element_type.72) | copy-start | bytes 4718596
  92.3 4.9 %copy-start.5 = (f32[3,256,256]{2,1,0:T(8,128)S(1)}, f32[3,256,256]{2,1,0:T(8,128)}, u32[]{:S(2)}) copy-start(f32[3,256,256]{2,1,0:T(8,128)} %copy-done.4) | copy-start | bytes 2359300
  92.3 4.9 %copy-start.20 = (f32[256,64]{0,1:T(8,128)S(1)}, f32[256,64]{0,1:T(8,128)}, u32[]{:S(2)}) copy-start(f32[256,64]{0,1:T(8,128)} %copy-done.19) | copy-start | bytes 196612
  92.3 6.6 %copy-start.11 = (f32[256,256]{0,1:T(8,128)S(1)}, f32[256,256]{0,1:T(8,128)}, u32[]{:S(2)}) copy-start(f32[256,256]{0,1:T(8,128)} %copy.15) | copy-start | bytes 786436
  92.3 6.6 %copy-start.18 = (f32[256,64]{0,1:T(8,128)S(1)}, f32[256,64]{0,1:T(8,128)}, u32[]{:S(2)}) copy-start(f32[256,64]{0,1:T(8,128)} %copy-done.17) | copy-start | bytes 196612
  96.8 4.3 %copy-start.10 = (bf16[4,256,256]{2,1,0:T(8,128)(2,1)S(1)}, bf16[4,256,256]{2,1,0:T(8,128)(2,1)}, u32[]{:S(2)}) copy-start(bf16[4,256,256]{2,1,0:T(8,128)(2,1)} %param.17) | copy-start | bytes 1572868
  101.8 1.2 copy-start.3
  101.8 1.5 %copy-start.8 = (f32[4096,64]{0,1:T(8,128)S(1)}, f32[4096,64]{0,1:T(8,128)}, u32[]{:S(2)}) copy-start(f32[4096,64]{0,1:T(8,128)} %param.13) | copy-start | bytes 3145732
  101.8 1.6 %copy-start.13 = (f32[1024,64]{0,1:T(8,128)S(1)}, f32[1024,64]{0,1:T(8,128)}, u32[]{:S(2)}) copy-start(f32[1024,64]{0,1:T(8,128)} %fusion.10) | copy-start | bytes 786436
  101.8 1.6 %copy-start.14 = (f32[1024,64]{0,1:T(8,128)S(1)}, f32[1024,64]{0,1:T(8,128)}, u32[]{:S(2)}) copy-start(f32[1024,64]{0,1:T(8,128)} %fusion.12) | copy-start | bytes 786436
  101.8 1.7 %copy-start.15 = (f32[1024,64]{0,1:T(8,128)S(1)}, f32[1024,64]{0,1:T(8,128)}, u32[]{:S(2)}) copy-start(f32[1024,64]{0,1:T(8,128)} %fusion.13) | copy-start | bytes 786436
  101.8 1.8 %copy-start.16 = (f32[1024,64]{0,1:T(8,128)S(1)}, f32[1024,64]{0,1:T(8,128)}, u32[]{:S(2)}) copy-start(f32[1024,64]{0,1:T(8,128)} %fusion.11) | copy-start | bytes 786436
